TPU v7x, 128 devices: a whole 4x4x4 slice. The times are simulated.
128 devices in a mesh: cuts: 8 (over x_lo, z), dom: 16 (over y, x_hi, core).
Axes of the slice: x: 4 (x_hi: 2, x_lo: 2; x = x_hi * 2 + x_lo), y: 4, z: 4, core: 2. Of those that a mesh axis runs over, the one named last changes fastest.
Arguments:
- radiation: float32 [256, 16, 512], P('dom', 'cuts'), may hold values from -6 to 6
- electrons: float32 [2, 16, 32768], P(None, 'cuts', 'dom'), may hold values from -6 to 6
- cell_index: int32 [2, 16, 32768], P(None, 'cuts', 'dom'), may hold values from 0 to 254
- cell_offset: float32 [2, 16, 32768], P(None, 'cuts', 'dom'), may hold values from 0 to 1
- kernel_x: float32 [2, 256, 256], replicated, may hold values from -0.25 to 0.25
- kernel_y: float32 [2, 256, 256], replicated, may hold values from -0.25 to 0.25
Outputs:
- radiation_out: float32 [256, 16, 512], P('dom', 'cuts')
- electrons_out: float32 [2, 16, 32768], P(None, 'cuts', 'dom')
Inputs may be any that keep to these rules, and one draw needn't show every extreme that they name: `cell_index`: the field is interpolated between cell and cell + 1 in each dimension, so every index stays below 255.
All inputs are finite; a program needn't handle non-finite values.
Results may differ from a plain program's by a relative error of at most 0.0003.
Values sent between devices are 32-bit elements; how exact they have to be, the bound alone decides.
A program may use at most 64 MiB of HBM per device.

v0:
```python
import jax
import jax.numpy as jnp
from jax import lax
from jax.experimental import pallas as pl
from jax.experimental.pallas import tpu as pltpu
from jax.sharding import PartitionSpec as P

ITERS = 4
SLICES = 16
coupling = 0.5
phase_step = 1.0
current_gain = 1.0
MESH = pl.DeviceIdType.MESH
f32 = jnp.float32
bf16 = jnp.bfloat16

BLOCKS = 4
ROWS = 8
LANES = 256


def split(value):
    hi = value.astype(bf16)
    return hi, (value - hi.astype(f32)).astype(bf16)


def mm(a, b):
    return jnp.dot(a, b, preferred_element_type=f32)


def mm_nt(a, b):
    return lax.dot_general(a, b, (((1,), (1,)), ((), ())), preferred_element_type=f32)


def role_device(number, y, core):
    pair = number // 2
    x_hi, z = pair // 4, pair % 4
    x_lo = (number % 2 + z + x_hi) % 2
    return x_lo * 4 + z, y * 4 + x_hi * 2 + core


def home_device(number, x_hi, y, core):
    return number // 2, y * 4 + x_hi * 2 + core


def kernel(
    rad,
    el_in,
    kx,
    ky,
    rad_out,
    el_out,
    el,
    wx,
    wy,
    field,
    shift,
    a_send,
    a_recv,
    trig,
    v_hi,
    v_lo,
    current,
    k2,
    big_y,
    mixed,
    sums,
    p_send,
    p_out,
    el_send,
    init_send,
    el_sem,
    row_send,
    row_sem,
    ag_send,
    ag_sem,
    a_ssem,
    a_rsem,
    rs_send,
    rs_sem,
    sh_send,
    sh_sem,
    out_send,
    out_sem,
):
    cuts, dom = lax.axis_index("cuts"), lax.axis_index("dom")
    x_lo, z = cuts // 4, cuts % 4
    y, x_hi, core = dom // 4, dom // 2 % 2, dom % 2
    number = 2 * (x_hi * 4 + z) + (x_lo + z + x_hi) % 2
    q = y * 2 + core
    following = (number + 1) % SLICES

    def remote(src, dst, ssem, rsem, device):
        return pltpu.make_async_remote_copy(
            src_ref=src,
            dst_ref=dst,
            send_sem=ssem,
            recv_sem=rsem,
            device_id=device,
            device_id_type=MESH,
        )

    def send(src, dst, ssem, rsem, device):
        self_target = jnp.logical_and(device[0] == cuts, device[1] == dom)

        @pl.when(self_target)
        def _():
            pltpu.make_async_copy(src, dst, rsem).start()

        @pl.when(jnp.logical_not(self_target))
        def _():
            remote(src, dst, ssem, rsem, device).start()

    def sent(src, dst, ssem, rsem, device):
        self_target = jnp.logical_and(device[0] == cuts, device[1] == dom)

        @pl.when(jnp.logical_not(self_target))
        def _():
            remote(src, dst, ssem, rsem, device).wait_send()

    def received(dst, rsem):
        pltpu.make_async_copy(dst, dst, rsem).wait()

    own_slot = x_hi * 2 + core
    starts = []
    for p in range(2):
        target = role_device(2 * cuts + p, y, core)
        other = role_device(2 * cuts + p, y, 1 - core)
        starts.append(
            (el_in.at[p], el.at[own_slot], init_send.at[p, 0], el_sem.at[own_slot], target)
        )
        starts.append(
            (el_in.at[p], el.at[own_slot], init_send.at[p, 1], el_sem.at[own_slot], other)
        )
        starts.append(
            (rad.at[p], shift.at[0, :, x_hi], row_send.at[p], row_sem.at[x_hi], target)
        )
    for args in starts:
        send(*args)

    kr, ki = kx[0], kx[1]
    for number_part, part in enumerate(split(jnp.concatenate([kr, ki], axis=1))):
        k2[number_part] = part
    for half_in in range(2):
        for half_out in range(2):
            block_re = ky[0, half_in * 128 : half_in * 128 + 128, half_out * 128 : half_out * 128 + 128]
            block_im = ky[1, half_in * 128 : half_in * 128 + 128, half_out * 128 : half_out * 128 + 128]
            rows = jnp.concatenate(
                [
                    jnp.concatenate([block_re, block_im], axis=1),
                    jnp.concatenate([-block_im, block_re], axis=1),
                ],
                axis=0,
            )
            for number_part, part in enumerate(split(rows)):
                big_y[
                    number_part,
                    half_in * 256 : half_in * 256 + 256,
                    half_out * 256 : half_out * 256 + 256,
                ] = part

    for slot in range(BLOCKS):
        received(el.at[slot], el_sem.at[slot])
    for part in range(2):
        received(shift.at[0, :, part], row_sem.at[part])

    grid_x = lax.broadcasted_iota(jnp.int32, (256, LANES), 0).astype(f32)
    grid_y = (lax.broadcasted_iota(jnp.int32, (128, LANES), 0) + core * 128).astype(f32)

    @pl.loop(0, BLOCKS)
    def _(block):
        for row in range(ROWS):
            index_x = el[block, 2, row : row + 1, :]
            index_y = el[block, 3, row : row + 1, :]
            offset_x = el[block, 4, row : row + 1, :]
            offset_y = el[block, 5, row : row + 1, :]
            lanes = slice(row * LANES, row * LANES + LANES)
            weight = jnp.where(grid_x == index_x, 1.0 - offset_x, 0.0) + jnp.where(
                grid_x == index_x + 1.0, offset_x, 0.0
            )
            hi, lo = split(weight)
            wx[block, 0:256, lanes] = hi
            wx[block, 256:512, lanes] = lo
            wy[block, :, lanes] = jnp.where(grid_y == index_y, 1.0 - offset_y, 0.0) + jnp.where(
                grid_y == index_y + 1.0, offset_y, 0.0
            )
        trig[block, 0] = jnp.cos(el[block, 0])
        trig[block, 1] = jnp.sin(el[block, 0])

    def peer(step):
        other = (q + step) % 8
        return other // 2, other % 2

    def source(step):
        other = (q + 8 - step) % 8
        return other // 2, other % 2

    def gather_copy(n, step):
        to_y, to_core = peer(step)
        return remote(
            shift.at[n, to_core],
            field.at[y, :, core],
            ag_send.at[step],
            ag_sem.at[step],
            role_device(number, to_y, to_core),
        )

    def sums_copy(step):
        to_y, to_core = peer(step)
        return remote(
            mixed.at[to_y, :, to_core],
            sums.at[q],
            rs_send.at[step],
            rs_sem.at[step],
            role_device(number, to_y, to_core),
        )

    def a_copy(block):
        return remote(
            a_send.at[block],
            a_recv.at[block],
            a_ssem.at[block],
            a_rsem.at[block],
            role_device(number, y, 1 - core),
        )

    def out_electrons(part):
        return (
            el_send.at[part],
            el_out.at[number % 2],
            out_send.at[2 + part],
            out_sem.at[2 + number % 2],
            home_device(number, part, y, core),
        )

    def advance(n, last):
        for step in range(1, 8):
            gather_copy(n, step).start()
        field[y, :, core] = shift[n, core]
        for step in range(1, 8):
            from_y, from_core = source(step)
            received(field.at[from_y, :, from_core], ag_sem.at[step])
        full = field[...].reshape(256, 256)
        hi, lo = split(full.T)
        both = jnp.concatenate([hi, lo], axis=0)

        @pl.loop(0, BLOCKS)
        def _(block):
            for row in range(ROWS):
                lanes = slice(row * LANES, row * LANES + LANES)
                first = mm(both, wx[block, 0:256, lanes])
                second = mm(both[0:256], wx[block, 256:512, lanes])
                values = first[0:256] + first[256:512] + second
                weight = wy[block, :, lanes]
                a_send[block, 0, row : row + 1, :] = jnp.sum(
                    values[0:128] * weight, axis=0, keepdims=True
                )
                a_send[block, 1, row : row + 1, :] = jnp.sum(
                    values[128:256] * weight, axis=0, keepdims=True
                )
            a_copy(block).start()

        current[...] = 0.25 * full

        @pl.loop(0, BLOCKS)
        def _(block):
            received(a_recv.at[block], a_rsem.at[block])
            a_re = a_send[block, 0] + a_recv[block, 0]
            a_im = a_send[block, 1] + a_recv[block, 1]
            energy = el[block, 1] - coupling * (a_re * trig[block, 0] - a_im * trig[block, 1])
            phase = el[block, 0] + phase_step * energy
            el[block, 0] = phase
            el[block, 1] = energy
            cos, sin = jnp.cos(phase), jnp.sin(phase)
            trig[block, 0] = cos
            trig[block, 1] = sin
            for row in range(ROWS):
                lanes = slice(row * LANES, row * LANES + LANES)
                weight = current_gain * wy[block, :, lanes]
                values = jnp.concatenate(
                    [weight * cos[row : row + 1, :], -weight * sin[row : row + 1, :]], axis=0
                )
                hi, lo = split(values)
                v_hi[:, lanes] = hi
                v_lo[:, lanes] = lo
            first = mm_nt(wx[block], v_hi[...])
            second = mm_nt(wx[block, 0:256], v_lo[...])
            current[...] += first[0:256] + first[256:512] + second

        if last:
            for part in range(2):
                el_send[part] = el[part * 2 + core, 0:2]
                send(*out_electrons(part))

        total = current[...]
        re, im = total[:, 0:128], total[:, 128:256]
        stacked = jnp.concatenate(
            [total, jnp.concatenate([-im, re], axis=1)], axis=0
        )
        hi, lo = split(stacked)
        product = mm(k2[0], hi) + mm(k2[1], hi) + mm(k2[0], lo)
        mixed[...] = product.reshape(mixed.shape)
        for step in range(1, 8):
            sums_copy(step).start()
        sums[q] = mixed[y, :, core]
        for step in range(1, 8):
            from_y, from_core = source(step)
            received(sums.at[from_y * 2 + from_core], rs_sem.at[step])
        halves = [
            ((sums[half] + sums[half + 2]) + (sums[half + 4] + sums[half + 6])).reshape(32, 256)
            for half in range(2)
        ]
        hi, lo = split(jnp.concatenate(halves, axis=1))
        result = mm(hi, big_y[0]) + mm(hi, big_y[1]) + mm(lo, big_y[0])
        result = jnp.where(following == 0, 0.0, result)
        if last:
            p_out[...] = jnp.concatenate(
                [result[:, 0:128], result[:, 256:384], result[:, 128:256], result[:, 384:512]],
                axis=1,
            ).reshape(p_out.shape)
        else:
            for half in range(2):
                p_send[half] = result[:, half * 256 : half * 256 + 256].reshape(2, 16, 256)
            copy = remote(
                p_send,
                shift.at[n + 1],
                sh_send.at[n],
                sh_sem.at[n],
                role_device(following, y, core),
            )
            copy.start()
        for step in range(1, 8):
            gather_copy(n, step).wait_send()
            sums_copy(step).wait_send()

        @pl.loop(0, BLOCKS)
        def _(block):
            a_copy(block).wait_send()

        if not last:
            copy.wait_send()
            received(shift.at[n + 1], sh_sem.at[n])

    @pl.loop(0, ITERS - 1)
    def _(n):
        advance(n, False)

    advance(ITERS - 1, True)

    def out_rows(part):
        return (
            p_out.at[part],
            rad_out.at[following % 2],
            out_send.at[part],
            out_sem.at[following % 2],
            home_device(following, part, y, core),
        )

    for part in range(2):
        send(*out_rows(part))
    for args in starts:
        sent(*args)
    for part in range(2):
        sent(*out_rows(part))
        sent(*out_electrons(part))
    for part in range(2):
        received(rad_out.at[part], out_sem.at[part])
        received(el_out.at[part], out_sem.at[2 + part])


def shards(radiation, electrons, cell_index, cell_offset, kernel_x, kernel_y):
    rad = radiation.reshape(16, 2, 2, 2, 128).transpose(1, 3, 0, 2, 4).reshape(2, 2, 16, 256)
    el_in = jnp.concatenate([electrons, cell_index.astype(f32), cell_offset], axis=0)
    el_in = el_in.transpose(1, 0, 2).reshape(2, 6, ROWS, LANES)
    vmem = pl.BlockSpec(memory_space=pltpu.VMEM)
    dma = pltpu.SemaphoreType.DMA
    rad_out, el_out = pl.pallas_call(
        kernel,
        out_shape=(
            jax.ShapeDtypeStruct((2, 16, 512), f32),
            jax.ShapeDtypeStruct((2, 2, ROWS, LANES), f32),
        ),
        in_specs=[vmem] * 4,
        out_specs=(vmem, vmem),
        scratch_shapes=[
            pltpu.VMEM((BLOCKS, 6, ROWS, LANES), f32),
            pltpu.VMEM((BLOCKS, 512, ROWS * LANES), bf16),
            pltpu.VMEM((BLOCKS, 128, ROWS * LANES), f32),
            pltpu.VMEM((4, 2, 2, 16, 256), f32),
            pltpu.VMEM((ITERS, 2, 2, 16, 256), f32),
            pltpu.VMEM((BLOCKS, 2, ROWS, LANES), f32),
            pltpu.VMEM((BLOCKS, 2, ROWS, LANES), f32),
            pltpu.VMEM((BLOCKS, 2, ROWS, LANES), f32),
            pltpu.VMEM((256, ROWS * LANES), bf16),
            pltpu.VMEM((256, ROWS * LANES), bf16),
            pltpu.VMEM((256, 256), f32),
            pltpu.VMEM((2, 256, 512), bf16),
            pltpu.VMEM((2, 512, 512), bf16),
            pltpu.VMEM((4, 2, 2, 16, 256), f32),
            pltpu.VMEM((8, 2, 16, 256), f32),
            pltpu.VMEM((2, 2, 16, 256), f32),
            pltpu.VMEM((2, 16, 512), f32),
            pltpu.VMEM((2, 2, ROWS, LANES), f32),
            dma((2, 2)),
            dma((BLOCKS,)),
            dma((2,)),
            dma((2,)),
            dma((8,)),
            dma((8,)),
            dma((BLOCKS,)),
            dma((BLOCKS,)),
            dma((8,)),
            dma((8,)),
            dma((ITERS,)),
            dma((ITERS,)),
            dma((4,)),
            dma((4,)),
        ],
        compiler_params=pltpu.CompilerParams(
            has_side_effects=True, vmem_limit_bytes=48 * 1024 * 1024
        ),
    )(rad, el_in, kernel_x, kernel_y)
    radiation_out = rad_out.transpose(1, 0, 2)
    electrons_out = el_out.reshape(2, 2, ROWS * LANES).transpose(1, 0, 2)
    return radiation_out, electrons_out


def solution(mesh):
    placed = (
        P("dom", "cuts", None),
        P(None, "cuts", "dom"),
        P(None, "cuts", "dom"),
        P(None, "cuts", "dom"),
        P(),
        P(),
    )
    return jax.shard_map(
        shards,
        mesh=mesh,
        in_specs=placed,
        out_specs=(P("dom", "cuts", None), P(None, "cuts", "dom")),
        check_vma=False,
    )
```

profile of v0, /device:TPU:1, one launch (start us, length us, event | category | flops | bytes accessed | tf_op | source)
XLA Modules:
  0.0 120.3 jit_solution(5091548978330103983)
XLA Ops:
  0.6 0.0 copy-start.1
  0.6 0.0 copy-start
  0.7 0.9 convert_element_type.3
  1.5 0.8 maximum_bitcast_fusion
  2.3 0.1 reshape.18
  2.4 0.9 reshape.16
  3.4 0.1 reshape.17.rad
  3.5 0.0 copy-done.1
  3.5 0.0 copy-done
  3.5 115.5 %shard_map.77 = (f32[2,16,512]{2,1,0:T(8,128)S(1)}, f32[2,2,8,256]{3,2,1,0:T(8,128)S(1)}) custom-call(f32[2,2,16,256]{3,2,1,0:T(8,128)S(1)} %reshape.17.rad, f32[2,6,8,256]{3,2,1,0:T(8,128)S(1)} %copy.13.el_in, f32[2,256,256]{2,1,0:T(8,128)S(1)} %copy-done, f32[2,256,256]{2,1,0:T(8,128)S(1)} %copy-done.1), custom_call_target="tpu_custom_call" | custom-call | tf_op jit(solution)/shard_map/pallas_call | solution.py:377
  119.0 0.7 copy.15
  119.7 0.6 copy.19
  (3 shorter events, 0.1 us)
Async XLA Ops:
  0.6 2.8 %copy-start.1 = (f32[2,256,256]{2,1,0:T(8,128)S(1)}, f32[2,256,256]{2,1,0:T(8,128)}, u32[]{:S(2)}) copy-start(f32[2,256,256]{2,1,0:T(8,128)} %ky.1) | copy-start | bytes 1572868
  0.6 2.8 %copy-start = (f32[2,256,256]{2,1,0:T(8,128)S(1)}, f32[2,256,256]{2,1,0:T(8,128)}, u32[]{:S(2)}) copy-start(f32[2,256,256]{2,1,0:T(8,128)} %kx.1) | copy-start | bytes 1572868
where the time goes:
time: 121 us; the launch traced here: 120 us
  Pallas kernels  115 us (95%)
  local copies, waits for them, and re-layouts  2.45 us (2%)
  other arithmetic  1.68 us (1%)
    pallas_call x1, Pallas kernels, shards(): pl.pallas_call(kernel, out_shape=(jax.ShapeDtypeStruct((2, 16, 512), f32)...  115 us

commit v1 on v0

--- a/solution.py
+++ b/solution.py
@@ -17,6 +17,13 @@
 BLOCKS = 4
 ROWS = 8
 LANES = 256
+ROW_BLOCKS = [
+    ((w * 2 + (t + y_lo) % 2) * 2 + core, t)
+    for t in range(2)
+    for y_lo in range(2)
+    for w in range(2)
+    for core in range(2)
+]
 
 
 def split(value):
@@ -32,24 +39,31 @@
     return lax.dot_general(a, b, (((1,), (1,)), ((), ())), preferred_element_type=f32)
 
 
-def role_device(number, y, core):
+def role_device(number, w, u, core):
     pair = number // 2
     x_hi, z = pair // 4, pair % 4
-    x_lo = (number % 2 + z + x_hi) % 2
-    return x_lo * 4 + z, y * 4 + x_hi * 2 + core
-
-
-def home_device(number, x_hi, y, core):
-    return number // 2, y * 4 + x_hi * 2 + core
+    y_hi = (number % 2 + z) % 2
+    x_lo, y_lo = (w + x_hi) % 2, (u + y_hi) % 2
+    return x_lo * 4 + z, (y_hi * 2 + y_lo) * 4 + x_hi * 2 + core
+
+
+def home_device(number, w, t, u, core):
+    return number // 2, (t * 2 + (u + t) % 2) * 4 + w * 2 + core
 
 
 def kernel(
+    radiation,
+    electrons,
+    cell_index,
+    cell_offset,
+    kx,
+    ky,
+    radiation_out,
+    electrons_out,
     rad,
     el_in,
-    kx,
-    ky,
-    rad_out,
-    el_out,
+    rad_back,
+    el_back,
     el,
     wx,
     wy,
@@ -86,9 +100,15 @@
     cuts, dom = lax.axis_index("cuts"), lax.axis_index("dom")
     x_lo, z = cuts // 4, cuts % 4
     y, x_hi, core = dom // 4, dom // 2 % 2, dom % 2
-    number = 2 * (x_hi * 4 + z) + (x_lo + z + x_hi) % 2
-    q = y * 2 + core
+    y_hi = y // 2
+    w, u = (x_lo + x_hi) % 2, (y + y_hi) % 2
+    number = 2 * (x_hi * 4 + z) + (y_hi + z) % 2
+    q = (w * 2 + u) * 2 + core
     following = (number + 1) % SLICES
+    previous = (number + SLICES - 1) % SLICES
+
+    def peer_device(other):
+        return role_device(number, other // 4, other // 2 % 2, other % 2)
 
     def remote(src, dst, ssem, rsem, device):
         return pltpu.make_async_remote_copy(
@@ -121,20 +141,67 @@
     def received(dst, rsem):
         pltpu.make_async_copy(dst, dst, rsem).wait()
 
-    own_slot = x_hi * 2 + core
+    greeted = [peer_device((q + step) % 8) for step in range(1, 8)]
+    for a in range(2):
+        greeted.append(role_device(2 * cuts + a, x_hi, u, core))
+        greeted.append(role_device(2 * cuts + a, x_hi, u, 1 - core))
+        greeted.append(home_device(number, w, a, u, core))
+        greeted.append(home_device(number, w, a, u, 1 - core))
+        greeted.append(home_device(following, w, a, u, core))
+        greeted.append(role_device((2 * cuts + a + SLICES - 1) % SLICES, x_hi, u, core))
+    greeted.append(role_device(following, w, u, core))
+    greeted.append(role_device(previous, w, u, core))
+    barrier = pltpu.get_barrier_semaphore()
+    expected = 0
+    for device in greeted:
+        others = jnp.logical_or(device[0] != cuts, device[1] != dom)
+        expected = expected + others.astype(jnp.int32)
+
+        @pl.when(others)
+        def _():
+            pl.semaphore_signal(barrier, inc=1, device_id=device, device_id_type=MESH)
+
+    for p in range(2):
+        for half in range(2):
+            for part in range(2):
+                column = part * 256 + half * 128
+                rad[p, half, :, part * 128 : part * 128 + 128] = radiation[
+                    :, p, column : column + 128
+                ]
+        for row in range(ROWS):
+            lanes = slice(row * LANES, row * LANES + LANES)
+            for field_number in range(2):
+                place = slice(row, row + 1)
+                el_in[p, field_number, place] = electrons[field_number, p : p + 1, lanes]
+                el_in[p, 2 + field_number, place] = cell_index[
+                    field_number, p : p + 1, lanes
+                ].astype(f32)
+                el_in[p, 4 + field_number, place] = cell_offset[field_number, p : p + 1, lanes]
+    pl.semaphore_wait(barrier, expected)
+
+    own_slot = y_hi * 2 + core
     starts = []
     for p in range(2):
-        target = role_device(2 * cuts + p, y, core)
-        other = role_device(2 * cuts + p, y, 1 - core)
         starts.append(
-            (el_in.at[p], el.at[own_slot], init_send.at[p, 0], el_sem.at[own_slot], target)
-        )
-        starts.append(
-            (el_in.at[p], el.at[own_slot], init_send.at[p, 1], el_sem.at[own_slot], other)
-        )
-        starts.append(
-            (rad.at[p], shift.at[0, :, x_hi], row_send.at[p], row_sem.at[x_hi], target)
-        )
+            (
+                rad.at[p],
+                shift.at[0, :, y_hi],
+                row_send.at[p],
+                row_sem.at[y_hi],
+                role_device(2 * cuts + p, x_hi, u, core),
+            )
+        )
+    for p in range(2):
+        for number_core in range(2):
+            starts.append(
+                (
+                    el_in.at[p],
+                    el.at[own_slot],
+                    init_send.at[p, number_core],
+                    el_sem.at[own_slot],
+                    role_device(2 * cuts + p, x_hi, u, (core + number_core) % 2),
+                )
+            )
     for args in starts:
         send(*args)
 
@@ -159,61 +226,32 @@
                     half_out * 256 : half_out * 256 + 256,
                 ] = part
 
-    for slot in range(BLOCKS):
-        received(el.at[slot], el_sem.at[slot])
-    for part in range(2):
-        received(shift.at[0, :, part], row_sem.at[part])
-
-    grid_x = lax.broadcasted_iota(jnp.int32, (256, LANES), 0).astype(f32)
-    grid_y = (lax.broadcasted_iota(jnp.int32, (128, LANES), 0) + core * 128).astype(f32)
-
-    @pl.loop(0, BLOCKS)
-    def _(block):
-        for row in range(ROWS):
-            index_x = el[block, 2, row : row + 1, :]
-            index_y = el[block, 3, row : row + 1, :]
-            offset_x = el[block, 4, row : row + 1, :]
-            offset_y = el[block, 5, row : row + 1, :]
-            lanes = slice(row * LANES, row * LANES + LANES)
-            weight = jnp.where(grid_x == index_x, 1.0 - offset_x, 0.0) + jnp.where(
-                grid_x == index_x + 1.0, offset_x, 0.0
-            )
-            hi, lo = split(weight)
-            wx[block, 0:256, lanes] = hi
-            wx[block, 256:512, lanes] = lo
-            wy[block, :, lanes] = jnp.where(grid_y == index_y, 1.0 - offset_y, 0.0) + jnp.where(
-                grid_y == index_y + 1.0, offset_y, 0.0
-            )
-        trig[block, 0] = jnp.cos(el[block, 0])
-        trig[block, 1] = jnp.sin(el[block, 0])
-
     def peer(step):
-        other = (q + step) % 8
-        return other // 2, other % 2
+        return (q + step) % 8
 
     def source(step):
-        other = (q + 8 - step) % 8
-        return other // 2, other % 2
+        return (q + 8 - step) % 8
 
     def gather_copy(n, step):
-        to_y, to_core = peer(step)
+        to = peer(step)
         return remote(
-            shift.at[n, to_core],
-            field.at[y, :, core],
+            shift.at[n, to % 2],
+            field.at[q],
             ag_send.at[step],
             ag_sem.at[step],
-            role_device(number, to_y, to_core),
+            peer_device(to),
         )
 
     def sums_copy(step):
-        to_y, to_core = peer(step)
+        to = peer(step)
         return remote(
-            mixed.at[to_y, :, to_core],
-            sums.at[q],
-            rs_send.at[step],
-            rs_sem.at[step],
-            role_device(number, to_y, to_core),
-        )
+            mixed.at[to], sums.at[q], rs_send.at[step], rs_sem.at[step], peer_device(to)
+        )
+
+    def start_gather(n):
+        for step in range(1, 8):
+            gather_copy(n, step).start()
+        field[q] = shift[n, core]
 
     def a_copy(block):
         return remote(
@@ -221,26 +259,22 @@
             a_recv.at[block],
             a_ssem.at[block],
             a_rsem.at[block],
-            role_device(number, y, 1 - core),
+            role_device(number, w, u, 1 - core),
         )
 
     def out_electrons(part):
         return (
             el_send.at[part],
-            el_out.at[number % 2],
+            el_back.at[number % 2],
             out_send.at[2 + part],
             out_sem.at[2 + number % 2],
-            home_device(number, part, y, core),
+            home_device(number, w, part, u, core),
         )
 
     def advance(n, last):
         for step in range(1, 8):
-            gather_copy(n, step).start()
-        field[y, :, core] = shift[n, core]
-        for step in range(1, 8):
-            from_y, from_core = source(step)
-            received(field.at[from_y, :, from_core], ag_sem.at[step])
-        full = field[...].reshape(256, 256)
+            received(field.at[source(step)], ag_sem.at[step])
+        full = jnp.concatenate([field[owner, part] for owner, part in ROW_BLOCKS], axis=0)
         hi, lo = split(full.T)
         both = jnp.concatenate([hi, lo], axis=0)
 
@@ -299,13 +333,13 @@
         )
         hi, lo = split(stacked)
         product = mm(k2[0], hi) + mm(k2[1], hi) + mm(k2[0], lo)
-        mixed[...] = product.reshape(mixed.shape)
+        for place, (owner, part) in enumerate(ROW_BLOCKS):
+            mixed[owner, part] = product[place * 16 : place * 16 + 16]
         for step in range(1, 8):
             sums_copy(step).start()
-        sums[q] = mixed[y, :, core]
+        sums[q] = mixed[q]
         for step in range(1, 8):
-            from_y, from_core = source(step)
-            received(sums.at[from_y * 2 + from_core], rs_sem.at[step])
+            received(sums.at[source(step)], rs_sem.at[step])
         halves = [
             ((sums[half] + sums[half + 2]) + (sums[half + 4] + sums[half + 6])).reshape(32, 256)
             for half in range(2)
@@ -326,7 +360,7 @@
                 shift.at[n + 1],
                 sh_send.at[n],
                 sh_sem.at[n],
-                role_device(following, y, core),
+                role_device(following, w, u, core),
             )
             copy.start()
         for step in range(1, 8):
@@ -340,6 +374,36 @@
         if not last:
             copy.wait_send()
             received(shift.at[n + 1], sh_sem.at[n])
+            start_gather(n + 1)
+
+    for part in range(2):
+        received(shift.at[0, :, part], row_sem.at[part])
+    start_gather(0)
+    for slot in range(BLOCKS):
+        received(el.at[slot], el_sem.at[slot])
+
+    grid_x = lax.broadcasted_iota(jnp.int32, (256, LANES), 0).astype(f32)
+    grid_y = (lax.broadcasted_iota(jnp.int32, (128, LANES), 0) + core * 128).astype(f32)
+
+    @pl.loop(0, BLOCKS)
+    def _(block):
+        for row in range(ROWS):
+            index_x = el[block, 2, row : row + 1, :]
+            index_y = el[block, 3, row : row + 1, :]
+            offset_x = el[block, 4, row : row + 1, :]
+            offset_y = el[block, 5, row : row + 1, :]
+            lanes = slice(row * LANES, row * LANES + LANES)
+            weight = jnp.where(grid_x == index_x, 1.0 - offset_x, 0.0) + jnp.where(
+                grid_x == index_x + 1.0, offset_x, 0.0
+            )
+            hi, lo = split(weight)
+            wx[block, 0:256, lanes] = hi
+            wx[block, 256:512, lanes] = lo
+            wy[block, :, lanes] = jnp.where(grid_y == index_y, 1.0 - offset_y, 0.0) + jnp.where(
+                grid_y == index_y + 1.0, offset_y, 0.0
+            )
+        trig[block, 0] = jnp.cos(el[block, 0])
+        trig[block, 1] = jnp.sin(el[block, 0])
 
     @pl.loop(0, ITERS - 1)
     def _(n):
@@ -350,10 +414,10 @@
     def out_rows(part):
         return (
             p_out.at[part],
-            rad_out.at[following % 2],
+            rad_back.at[following % 2],
             out_send.at[part],
             out_sem.at[following % 2],
-            home_device(following, part, y, core),
+            home_device(following, w, part, u, core),
         )
 
     for part in range(2):
@@ -364,29 +428,38 @@
         sent(*out_rows(part))
         sent(*out_electrons(part))
     for part in range(2):
-        received(rad_out.at[part], out_sem.at[part])
-        received(el_out.at[part], out_sem.at[2 + part])
+        received(rad_back.at[part], out_sem.at[part])
+        received(el_back.at[part], out_sem.at[2 + part])
+    for p in range(2):
+        radiation_out[:, p, :] = rad_back[p]
+        for row in range(ROWS):
+            lanes = slice(row * LANES, row * LANES + LANES)
+            for field_number in range(2):
+                electrons_out[field_number, p : p + 1, lanes] = el_back[
+                    p, field_number, row : row + 1
+                ]
 
 
 def shards(radiation, electrons, cell_index, cell_offset, kernel_x, kernel_y):
-    rad = radiation.reshape(16, 2, 2, 2, 128).transpose(1, 3, 0, 2, 4).reshape(2, 2, 16, 256)
-    el_in = jnp.concatenate([electrons, cell_index.astype(f32), cell_offset], axis=0)
-    el_in = el_in.transpose(1, 0, 2).reshape(2, 6, ROWS, LANES)
     vmem = pl.BlockSpec(memory_space=pltpu.VMEM)
     dma = pltpu.SemaphoreType.DMA
-    rad_out, el_out = pl.pallas_call(
+    return pl.pallas_call(
         kernel,
         out_shape=(
-            jax.ShapeDtypeStruct((2, 16, 512), f32),
-            jax.ShapeDtypeStruct((2, 2, ROWS, LANES), f32),
+            jax.ShapeDtypeStruct(radiation.shape, f32),
+            jax.ShapeDtypeStruct(electrons.shape, f32),
         ),
-        in_specs=[vmem] * 4,
+        in_specs=[vmem] * 6,
         out_specs=(vmem, vmem),
         scratch_shapes=[
+            pltpu.VMEM((2, 2, 16, 256), f32),
+            pltpu.VMEM((2, 6, ROWS, LANES), f32),
+            pltpu.VMEM((2, 16, 512), f32),
+            pltpu.VMEM((2, 2, ROWS, LANES), f32),
             pltpu.VMEM((BLOCKS, 6, ROWS, LANES), f32),
             pltpu.VMEM((BLOCKS, 512, ROWS * LANES), bf16),
             pltpu.VMEM((BLOCKS, 128, ROWS * LANES), f32),
-            pltpu.VMEM((4, 2, 2, 16, 256), f32),
+            pltpu.VMEM((8, 2, 16, 256), f32),
             pltpu.VMEM((ITERS, 2, 2, 16, 256), f32),
             pltpu.VMEM((BLOCKS, 2, ROWS, LANES), f32),
             pltpu.VMEM((BLOCKS, 2, ROWS, LANES), f32),
@@ -396,7 +469,7 @@
             pltpu.VMEM((256, 256), f32),
             pltpu.VMEM((2, 256, 512), bf16),
             pltpu.VMEM((2, 512, 512), bf16),
-            pltpu.VMEM((4, 2, 2, 16, 256), f32),
+            pltpu.VMEM((8, 2, 16, 256), f32),
             pltpu.VMEM((8, 2, 16, 256), f32),
             pltpu.VMEM((2, 2, 16, 256), f32),
             pltpu.VMEM((2, 16, 512), f32),
@@ -417,12 +490,9 @@
             dma((4,)),
         ],
         compiler_params=pltpu.CompilerParams(
-            has_side_effects=True, vmem_limit_bytes=48 * 1024 * 1024
+            collective_id=0, has_side_effects=True, vmem_limit_bytes=48 * 1024 * 1024
         ),
-    )(rad, el_in, kernel_x, kernel_y)
-    radiation_out = rad_out.transpose(1, 0, 2)
-    electrons_out = el_out.reshape(2, 2, ROWS * LANES).transpose(1, 0, 2)
-    return radiation_out, electrons_out
+    )(radiation, electrons, cell_index, cell_offset, kernel_x, kernel_y)
 
 
 def solution(mesh):

time: 121 us -> 113 us (0.934)
  Pallas kernels: 115 us -> 105 us
  local copies, waits for them, and re-layouts: 2.45 us -> 6.43 us
  other arithmetic: 1.68 us -> 0 us
    pallas_call x1, Pallas kernels: 115 us -> 105 us  [shards(): pl.pallas_call(kernel, out_shape=(jax.ShapeDtypeStruct(radiation.shape, f...]
    unnamed x5 -> x14, local copies, waits for them, and re-layouts: 0.69 us -> 6.43 us
    reshape x7 -> x0, local copies, waits for them, and re-layouts: 1.76 us -> none  [the longest x3 1.01 us: shards(): radiation.reshape(16, 2, 2, 2, 128).transpose(1, 3, 0, 2, 4)]
where the time goes in v1:
time: 113 us; the launch traced here: 112 us
  Pallas kernels  105 us (93%)
  local copies, waits for them, and re-layouts  6.43 us (6%)
    pallas_call x1, Pallas kernels, shards(): pl.pallas_call(kernel, out_shape=(jax.ShapeDtypeStruct(radiation.shape, f...  105 us
    unnamed x14, local copies, waits for them, and re-layouts  6.43 us

profile of v1, /device:TPU:1, one launch (start us, length us, event | category | flops | bytes accessed | tf_op | source)
XLA Modules:
  0.0 112.1 jit_solution(4152026328015308977)
XLA Ops:
  0.6 0.0 copy-start
  0.6 1.0 copy-done
  1.7 0.0 copy-start.1
  1.7 1.0 copy-done.1
  2.7 0.0 copy-start.2
  2.7 0.8 copy-done.2
  3.6 0.0 copy-start.3
  3.6 0.8 copy-done.3
  4.3 0.0 copy-start.4
  4.3 0.8 copy-done.4
  5.1 0.0 copy-start.5
  5.1 0.8 copy-done.5
  5.8 105.0 %shard_map.77 = (f32[16,2,512]{2,1,0:T(2,128)S(1)}, f32[2,2,2048]{2,1,0:T(2,128)S(1)}) custom-call(f32[16,2,512]{2,1,0:T(2,128)S(1)} %copy-done.2, f32[2,2,2048]{2,1,0:T(2,128)S(1)} %copy-done.3, s32[2,2,2048]{2,1,0:T(2,128)S(1)} %copy-done.4, f32[2,2,2048]{2,1,0:T(2,128)S(1)} %copy-done.5, f32[2,256,256]{2,1,0:T(8,128)S(1)} %copy-done, ...), custom_call_target="tpu_custom_call" | custom-call | tf_op jit(solution)/shard_map/pallas_call | solution.py:446
  110.8 0.6 copy.10
  111.5 0.6 copy.11
Async XLA Ops:
  0.6 1.0 copy-start
  1.7 1.0 copy-start.1
  2.7 0.8 copy-start.2
  3.6 0.8 copy-start.3
  4.3 0.8 copy-start.4
  5.1 0.8 copy-start.5

commit v2 on v1

--- a/solution.py
+++ b/solution.py
@@ -68,7 +68,6 @@
     wx,
     wy,
     field,
-    shift,
     a_send,
     a_recv,
     trig,
@@ -92,8 +91,10 @@
     a_rsem,
     rs_send,
     rs_sem,
-    sh_send,
-    sh_sem,
+    place_send,
+    place_sem,
+    state_send,
+    state_sem,
     out_send,
     out_sem,
 ):
@@ -104,11 +105,15 @@
     w, u = (x_lo + x_hi) % 2, (y + y_hi) % 2
     number = 2 * (x_hi * 4 + z) + (y_hi + z) % 2
     q = (w * 2 + u) * 2 + core
-    following = (number + 1) % SLICES
-    previous = (number + SLICES - 1) % SLICES
+    last_number = (number + ITERS - 1) % SLICES
+    row_number = (number + ITERS) % SLICES
 
     def peer_device(other):
         return role_device(number, other // 4, other // 2 % 2, other % 2)
+
+    peers = [peer_device((q + step) % 8) for step in range(8)]
+    beside = peer_device(q + 1 - 2 * core)
+    ahead = role_device((number + SLICES - 1) % SLICES, w, u, core)
 
     def remote(src, dst, ssem, rsem, device):
         return pltpu.make_async_remote_copy(
@@ -141,16 +146,17 @@
     def received(dst, rsem):
         pltpu.make_async_copy(dst, dst, rsem).wait()
 
-    greeted = [peer_device((q + step) % 8) for step in range(1, 8)]
+    greeted = peers[1:]
     for a in range(2):
         greeted.append(role_device(2 * cuts + a, x_hi, u, core))
         greeted.append(role_device(2 * cuts + a, x_hi, u, 1 - core))
         greeted.append(home_device(number, w, a, u, core))
         greeted.append(home_device(number, w, a, u, 1 - core))
-        greeted.append(home_device(following, w, a, u, core))
-        greeted.append(role_device((2 * cuts + a + SLICES - 1) % SLICES, x_hi, u, core))
-    greeted.append(role_device(following, w, u, core))
-    greeted.append(role_device(previous, w, u, core))
+        for moved, end in ((ITERS - 1, last_number), (ITERS, row_number)):
+            greeted.append(home_device(end, w, a, u, core))
+            greeted.append(role_device((2 * cuts + a + SLICES - moved) % SLICES, x_hi, u, core))
+    greeted.append(ahead)
+    greeted.append(role_device((number + 1) % SLICES, w, u, core))
     barrier = pltpu.get_barrier_semaphore()
     expected = 0
     for device in greeted:
@@ -185,7 +191,7 @@
         starts.append(
             (
                 rad.at[p],
-                shift.at[0, :, y_hi],
+                p_send.at[:, y_hi],
                 row_send.at[p],
                 row_sem.at[y_hi],
                 role_device(2 * cuts + p, x_hi, u, core),
@@ -196,7 +202,7 @@
             starts.append(
                 (
                     el_in.at[p],
-                    el.at[own_slot],
+                    el.at[0, own_slot],
                     init_send.at[p, number_core],
                     el_sem.at[own_slot],
                     role_device(2 * cuts + p, x_hi, u, (core + number_core) % 2),
@@ -226,54 +232,81 @@
                     half_out * 256 : half_out * 256 + 256,
                 ] = part
 
-    def peer(step):
-        return (q + step) % 8
-
-    def source(step):
-        return (q + 8 - step) % 8
-
-    def gather_copy(n, step):
-        to = peer(step)
+    def gather_copy(step):
         return remote(
-            shift.at[n, to % 2],
+            p_send.at[(core + step) % 2],
             field.at[q],
             ag_send.at[step],
             ag_sem.at[step],
-            peer_device(to),
+            peers[step],
         )
 
     def sums_copy(step):
-        to = peer(step)
         return remote(
-            mixed.at[to], sums.at[q], rs_send.at[step], rs_sem.at[step], peer_device(to)
-        )
-
-    def start_gather(n):
+            mixed.at[(q + step) % 8], sums.at[q], rs_send.at[step], rs_sem.at[step], peers[step]
+        )
+
+    def start_gather():
         for step in range(1, 8):
-            gather_copy(n, step).start()
-        field[q] = shift[n, core]
+            gather_copy(step).start()
+        field[q] = p_send[core]
 
     def a_copy(block):
         return remote(
-            a_send.at[block],
-            a_recv.at[block],
-            a_ssem.at[block],
-            a_rsem.at[block],
-            role_device(number, w, u, 1 - core),
+            a_send.at[block], a_recv.at[block], a_ssem.at[block], a_rsem.at[block], beside
+        )
+
+    def place_copy(n):
+        return remote(
+            el.at[n, :, 2:6], el.at[n + 1, :, 2:6], place_send.at[n], place_sem.at[n], ahead
+        )
+
+    def state_copy(n, block):
+        return remote(
+            el.at[n, block, 0:2],
+            el.at[n + 1, block, 0:2],
+            state_send.at[n, block],
+            state_sem.at[n, block],
+            ahead,
         )
 
     def out_electrons(part):
         return (
             el_send.at[part],
-            el_back.at[number % 2],
+            el_back.at[last_number % 2],
             out_send.at[2 + part],
-            out_sem.at[2 + number % 2],
-            home_device(number, w, part, u, core),
-        )
+            out_sem.at[2 + last_number % 2],
+            home_device(last_number, w, part, u, core),
+        )
+
+    def build(n):
+        @pl.loop(0, BLOCKS)
+        def _(block):
+            for row in range(ROWS):
+                index_x = el[n, block, 2, row : row + 1, :]
+                index_y = el[n, block, 3, row : row + 1, :]
+                offset_x = el[n, block, 4, row : row + 1, :]
+                offset_y = el[n, block, 5, row : row + 1, :]
+                lanes = slice(row * LANES, row * LANES + LANES)
+                grid_x = lax.broadcasted_iota(jnp.int32, (256, LANES), 0).astype(f32)
+                grid_y = (lax.broadcasted_iota(jnp.int32, (128, LANES), 0) + core * 128).astype(f32)
+                weight = jnp.where(grid_x == index_x, 1.0 - offset_x, 0.0) + jnp.where(
+                    grid_x == index_x + 1.0, offset_x, 0.0
+                )
+                hi, lo = split(weight)
+                wx[block, 0:256, lanes] = hi
+                wx[block, 256:512, lanes] = lo
+                wy[block, :, lanes] = jnp.where(
+                    grid_y == index_y, 1.0 - offset_y, 0.0
+                ) + jnp.where(grid_y == index_y + 1.0, offset_y, 0.0)
+            trig[block, 0] = jnp.cos(el[n, block, 0])
+            trig[block, 1] = jnp.sin(el[n, block, 0])
 
     def advance(n, last):
+        if not last:
+            place_copy(n).start()
         for step in range(1, 8):
-            received(field.at[source(step)], ag_sem.at[step])
+            received(field.at[(q + 8 - step) % 8], ag_sem.at[step])
         full = jnp.concatenate([field[owner, part] for owner, part in ROW_BLOCKS], axis=0)
         hi, lo = split(full.T)
         both = jnp.concatenate([hi, lo], axis=0)
@@ -301,13 +334,13 @@
             received(a_recv.at[block], a_rsem.at[block])
             a_re = a_send[block, 0] + a_recv[block, 0]
             a_im = a_send[block, 1] + a_recv[block, 1]
-            energy = el[block, 1] - coupling * (a_re * trig[block, 0] - a_im * trig[block, 1])
-            phase = el[block, 0] + phase_step * energy
-            el[block, 0] = phase
-            el[block, 1] = energy
+            energy = el[n, block, 1] - coupling * (a_re * trig[block, 0] - a_im * trig[block, 1])
+            phase = el[n, block, 0] + phase_step * energy
+            el[n, block, 0] = phase
+            el[n, block, 1] = energy
+            if not last:
+                state_copy(n, block).start()
             cos, sin = jnp.cos(phase), jnp.sin(phase)
-            trig[block, 0] = cos
-            trig[block, 1] = sin
             for row in range(ROWS):
                 lanes = slice(row * LANES, row * LANES + LANES)
                 weight = current_gain * wy[block, :, lanes]
@@ -323,30 +356,39 @@
 
         if last:
             for part in range(2):
-                el_send[part] = el[part * 2 + core, 0:2]
+                el_send[part] = el[n, part * 2 + core, 0:2]
                 send(*out_electrons(part))
 
         total = current[...]
         re, im = total[:, 0:128], total[:, 128:256]
-        stacked = jnp.concatenate(
-            [total, jnp.concatenate([-im, re], axis=1)], axis=0
-        )
+        stacked = jnp.concatenate([total, jnp.concatenate([-im, re], axis=1)], axis=0)
         hi, lo = split(stacked)
         product = mm(k2[0], hi) + mm(k2[1], hi) + mm(k2[0], lo)
-        for place, (owner, part) in enumerate(ROW_BLOCKS):
-            mixed[owner, part] = product[place * 16 : place * 16 + 16]
+        for index, (owner, part) in enumerate(ROW_BLOCKS):
+            mixed[owner, part] = product[index * 16 : index * 16 + 16]
         for step in range(1, 8):
             sums_copy(step).start()
         sums[q] = mixed[q]
+        if not last:
+            received(el.at[n + 1, :, 2:6], place_sem.at[n])
+
+            @pl.loop(0, BLOCKS)
+            def _(block):
+                received(el.at[n + 1, block, 0:2], state_sem.at[n, block])
+
+            build(n + 1)
         for step in range(1, 8):
-            received(sums.at[source(step)], rs_sem.at[step])
+            received(sums.at[(q + 8 - step) % 8], rs_sem.at[step])
         halves = [
             ((sums[half] + sums[half + 2]) + (sums[half + 4] + sums[half + 6])).reshape(32, 256)
             for half in range(2)
         ]
         hi, lo = split(jnp.concatenate(halves, axis=1))
         result = mm(hi, big_y[0]) + mm(hi, big_y[1]) + mm(lo, big_y[0])
-        result = jnp.where(following == 0, 0.0, result)
+        result = jnp.where((number + n + 1) % SLICES == 0, 0.0, result)
+        for step in range(1, 8):
+            gather_copy(step).wait_send()
+            sums_copy(step).wait_send()
         if last:
             p_out[...] = jnp.concatenate(
                 [result[:, 0:128], result[:, 256:384], result[:, 128:256], result[:, 384:512]],
@@ -355,55 +397,21 @@
         else:
             for half in range(2):
                 p_send[half] = result[:, half * 256 : half * 256 + 256].reshape(2, 16, 256)
-            copy = remote(
-                p_send,
-                shift.at[n + 1],
-                sh_send.at[n],
-                sh_sem.at[n],
-                role_device(following, w, u, core),
-            )
-            copy.start()
-        for step in range(1, 8):
-            gather_copy(n, step).wait_send()
-            sums_copy(step).wait_send()
+            start_gather()
+            place_copy(n).wait_send()
 
         @pl.loop(0, BLOCKS)
         def _(block):
             a_copy(block).wait_send()
-
-        if not last:
-            copy.wait_send()
-            received(shift.at[n + 1], sh_sem.at[n])
-            start_gather(n + 1)
+            if not last:
+                state_copy(n, block).wait_send()
 
     for part in range(2):
-        received(shift.at[0, :, part], row_sem.at[part])
-    start_gather(0)
+        received(p_send.at[:, part], row_sem.at[part])
+    start_gather()
     for slot in range(BLOCKS):
-        received(el.at[slot], el_sem.at[slot])
-
-    grid_x = lax.broadcasted_iota(jnp.int32, (256, LANES), 0).astype(f32)
-    grid_y = (lax.broadcasted_iota(jnp.int32, (128, LANES), 0) + core * 128).astype(f32)
-
-    @pl.loop(0, BLOCKS)
-    def _(block):
-        for row in range(ROWS):
-            index_x = el[block, 2, row : row + 1, :]
-            index_y = el[block, 3, row : row + 1, :]
-            offset_x = el[block, 4, row : row + 1, :]
-            offset_y = el[block, 5, row : row + 1, :]
-            lanes = slice(row * LANES, row * LANES + LANES)
-            weight = jnp.where(grid_x == index_x, 1.0 - offset_x, 0.0) + jnp.where(
-                grid_x == index_x + 1.0, offset_x, 0.0
-            )
-            hi, lo = split(weight)
-            wx[block, 0:256, lanes] = hi
-            wx[block, 256:512, lanes] = lo
-            wy[block, :, lanes] = jnp.where(grid_y == index_y, 1.0 - offset_y, 0.0) + jnp.where(
-                grid_y == index_y + 1.0, offset_y, 0.0
-            )
-        trig[block, 0] = jnp.cos(el[block, 0])
-        trig[block, 1] = jnp.sin(el[block, 0])
+        received(el.at[0, slot], el_sem.at[slot])
+    build(0)
 
     @pl.loop(0, ITERS - 1)
     def _(n):
@@ -414,10 +422,10 @@
     def out_rows(part):
         return (
             p_out.at[part],
-            rad_back.at[following % 2],
+            rad_back.at[row_number % 2],
             out_send.at[part],
-            out_sem.at[following % 2],
-            home_device(following, w, part, u, core),
+            out_sem.at[row_number % 2],
+            home_device(row_number, w, part, u, core),
         )
 
     for part in range(2):
@@ -456,11 +464,10 @@
             pltpu.VMEM((2, 6, ROWS, LANES), f32),
             pltpu.VMEM((2, 16, 512), f32),
             pltpu.VMEM((2, 2, ROWS, LANES), f32),
-            pltpu.VMEM((BLOCKS, 6, ROWS, LANES), f32),
+            pltpu.VMEM((ITERS, BLOCKS, 6, ROWS, LANES), f32),
             pltpu.VMEM((BLOCKS, 512, ROWS * LANES), bf16),
             pltpu.VMEM((BLOCKS, 128, ROWS * LANES), f32),
             pltpu.VMEM((8, 2, 16, 256), f32),
-            pltpu.VMEM((ITERS, 2, 2, 16, 256), f32),
             pltpu.VMEM((BLOCKS, 2, ROWS, LANES), f32),
             pltpu.VMEM((BLOCKS, 2, ROWS, LANES), f32),
             pltpu.VMEM((BLOCKS, 2, ROWS, LANES), f32),
@@ -486,6 +493,8 @@
             dma((8,)),
             dma((ITERS,)),
             dma((ITERS,)),
+            dma((ITERS, BLOCKS)),
+            dma((ITERS, BLOCKS)),
             dma((4,)),
             dma((4,)),
         ],

time: 113 us -> 107 us (0.947)
  Pallas kernels: 105 us -> 99.4 us
    pallas_call x1, Pallas kernels: 105 us -> 99.4 us  [shards(): pl.pallas_call(kernel, out_shape=(jax.ShapeDtypeStruct(radiation.shape, f...]
where the time goes in v2:
time: 107 us
  Pallas kernels  99.4 us (93%)
  local copies, waits for them, and re-layouts  6.43 us (6%)
    pallas_call x1, Pallas kernels, shards(): pl.pallas_call(kernel, out_shape=(jax.ShapeDtypeStruct(radiation.shape, f...  99.4 us
    unnamed x14, local copies, waits for them, and re-layouts  6.43 us

profile of v2, /device:TPU:1, one launch (start us, length us, event | category | flops | bytes accessed | tf_op | source)
XLA Modules:
  0.0 106.5 jit_solution(8314158901834588327)
XLA Ops:
  0.6 0.0 copy-start
  0.6 1.0 copy-done
  1.7 0.0 copy-start.1
  1.7 1.0 copy-done.1
  2.7 0.0 copy-start.2
  2.7 0.8 copy-done.2
  3.6 0.0 copy-start.3
  3.6 0.8 copy-done.3
  4.3 0.0 copy-start.4
  4.3 0.8 copy-done.4
  5.1 0.0 copy-start.5
  5.1 0.8 copy-done.5
  5.8 99.4 %shard_map.77 = (f32[16,2,512]{2,1,0:T(2,128)S(1)}, f32[2,2,2048]{2,1,0:T(2,128)S(1)}) custom-call(f32[16,2,512]{2,1,0:T(2,128)S(1)} %copy-done.2, f32[2,2,2048]{2,1,0:T(2,128)S(1)} %copy-done.3, s32[2,2,2048]{2,1,0:T(2,128)S(1)} %copy-done.4, f32[2,2,2048]{2,1,0:T(2,128)S(1)} %copy-done.5, f32[2,256,256]{2,1,0:T(8,128)S(1)} %copy-done, ...), custom_call_target="tpu_custom_call" | custom-call | tf_op jit(solution)/shard_map/pallas_call | solution.py:454
  105.3 0.6 copy.10
  105.9 0.6 copy.11
Async XLA Ops:
  0.6 1.0 copy-start
  1.7 1.0 copy-start.1
  2.7 0.8 copy-start.2
  3.6 0.8 copy-start.3
  4.3 0.8 copy-start.4
  5.1 0.8 copy-start.5

commit v3 on v2

--- a/solution.py
+++ b/solution.py
@@ -52,14 +52,20 @@
 
 
 def kernel(
+    radiation_hbm,
+    electrons_hbm,
+    cell_index_hbm,
+    cell_offset_hbm,
+    kx_hbm,
+    ky_hbm,
+    radiation_out,
+    electrons_out,
     radiation,
     electrons,
     cell_index,
     cell_offset,
     kx,
     ky,
-    radiation_out,
-    electrons_out,
     rad,
     el_in,
     rad_back,
@@ -97,6 +103,7 @@
     state_sem,
     out_send,
     out_sem,
+    in_sem,
 ):
     cuts, dom = lax.axis_index("cuts"), lax.axis_index("dom")
     x_lo, z = cuts // 4, cuts % 4
@@ -167,6 +174,23 @@
         def _():
             pl.semaphore_signal(barrier, inc=1, device_id=device, device_id_type=MESH)
 
+    loads = [
+        pltpu.make_async_copy(src, dst, in_sem.at[index])
+        for index, (src, dst) in enumerate(
+            [
+                (radiation_hbm, radiation),
+                (electrons_hbm, electrons),
+                (cell_index_hbm, cell_index),
+                (cell_offset_hbm, cell_offset),
+                (kx_hbm, kx),
+                (ky_hbm, ky),
+            ]
+        )
+    ]
+    for load in loads:
+        load.start()
+    for load in loads[0:4]:
+        load.wait()
     for p in range(2):
         for half in range(2):
             for part in range(2):
@@ -211,6 +235,8 @@
     for args in starts:
         send(*args)
 
+    for load in loads[4:6]:
+        load.wait()
     kr, ki = kx[0], kx[1]
     for number_part, part in enumerate(split(jnp.concatenate([kr, ki], axis=1))):
         k2[number_part] = part
@@ -457,9 +483,15 @@
             jax.ShapeDtypeStruct(radiation.shape, f32),
             jax.ShapeDtypeStruct(electrons.shape, f32),
         ),
-        in_specs=[vmem] * 6,
+        in_specs=[pl.BlockSpec(memory_space=pltpu.HBM)] * 6,
         out_specs=(vmem, vmem),
         scratch_shapes=[
+            pltpu.VMEM(radiation.shape, f32),
+            pltpu.VMEM(electrons.shape, f32),
+            pltpu.VMEM(cell_index.shape, jnp.int32),
+            pltpu.VMEM(cell_offset.shape, f32),
+            pltpu.VMEM(kernel_x.shape, f32),
+            pltpu.VMEM(kernel_y.shape, f32),
             pltpu.VMEM((2, 2, 16, 256), f32),
             pltpu.VMEM((2, 6, ROWS, LANES), f32),
             pltpu.VMEM((2, 16, 512), f32),
@@ -497,6 +529,7 @@
             dma((ITERS, BLOCKS)),
             dma((4,)),
             dma((4,)),
+            dma((6,)),
         ],
         compiler_params=pltpu.CompilerParams(
             collective_id=0, has_side_effects=True, vmem_limit_bytes=48 * 1024 * 1024

time: 107 us -> 107 us (level)
  no operation moved by 1% of the time
where the time goes in v3:
time: 107 us
  Pallas kernels  99.5 us (93%)
  local copies, waits for them, and re-layouts  6.43 us (6%)
    pallas_call x1, Pallas kernels, shards(): pl.pallas_call(kernel, out_shape=(jax.ShapeDtypeStruct(radiation.shape, f...  99.5 us
    unnamed x14, local copies, waits for them, and re-layouts  6.43 us

profile of v3, /device:TPU:1, one launch (start us, length us, event | category | flops | bytes accessed | tf_op | source)
XLA Modules:
  0.0 106.6 jit_solution(481183148086643222)
XLA Ops:
  0.6 0.0 copy-start
  0.6 1.0 copy-done
  1.7 0.0 copy-start.1
  1.7 1.0 copy-done.1
  2.7 0.0 copy-start.2
  2.7 0.8 copy-done.2
  3.6 0.0 copy-start.3
  3.6 0.8 copy-done.3
  4.3 0.0 copy-start.4
  4.3 0.8 copy-done.4
  5.1 0.0 copy-start.5
  5.1 0.8 copy-done.5
  5.8 99.5 %shard_map.77 = (f32[16,2,512]{2,1,0:T(2,128)S(1)}, f32[2,2,2048]{2,1,0:T(2,128)S(1)}) custom-call(f32[16,2,512]{2,1,0:T(2,128)S(1)} %copy-done.2, f32[2,2,2048]{2,1,0:T(2,128)S(1)} %copy-done.3, s32[2,2,2048]{2,1,0:T(2,128)S(1)} %copy-done.4, f32[2,2,2048]{2,1,0:T(2,128)S(1)} %copy-done.5, f32[2,256,256]{2,1,0:T(8,128)S(1)} %copy-done, ...), custom_call_target="tpu_custom_call" | custom-call | tf_op jit(solution)/shard_map/pallas_call | solution.py:480
  105.4 0.6 copy.10
  106.0 0.6 copy.11
Async XLA Ops:
  0.6 1.0 copy-start
  1.7 1.0 copy-start.1
  2.7 0.8 copy-start.2
  3.6 0.8 copy-start.3
  4.3 0.8 copy-start.4
  5.1 0.8 copy-start.5

commit v4 on v3

--- a/solution.py
+++ b/solution.py
@@ -13,10 +13,13 @@
 MESH = pl.DeviceIdType.MESH
 f32 = jnp.float32
 bf16 = jnp.bfloat16
+f8 = jnp.float8_e4m3fn
 
 BLOCKS = 4
 ROWS = 8
 LANES = 256
+LOW = 4096.0
+PEAK = 32.0
 ROW_BLOCKS = [
     ((w * 2 + (t + y_lo) % 2) * 2 + core, t)
     for t in range(2)
@@ -29,6 +32,11 @@
 def split(value):
     hi = value.astype(bf16)
     return hi, (value - hi.astype(f32)).astype(bf16)
+
+
+def split_low(value):
+    hi = value.astype(bf16)
+    return hi, ((value - hi.astype(f32)) * LOW).astype(f8)
 
 
 def mm(a, b):
@@ -79,6 +87,8 @@
     trig,
     v_hi,
     v_lo,
+    v_top,
+    w8,
     current,
     k2,
     big_y,
@@ -319,9 +329,10 @@
                 weight = jnp.where(grid_x == index_x, 1.0 - offset_x, 0.0) + jnp.where(
                     grid_x == index_x + 1.0, offset_x, 0.0
                 )
-                hi, lo = split(weight)
+                hi, lo = split_low(weight)
                 wx[block, 0:256, lanes] = hi
-                wx[block, 256:512, lanes] = lo
+                w8[block, 0:256, lanes] = weight.astype(f8)
+                w8[block, 256:512, lanes] = lo
                 wy[block, :, lanes] = jnp.where(
                     grid_y == index_y, 1.0 - offset_y, 0.0
                 ) + jnp.where(grid_y == index_y + 1.0, offset_y, 0.0)
@@ -334,21 +345,24 @@
         for step in range(1, 8):
             received(field.at[(q + 8 - step) % 8], ag_sem.at[step])
         full = jnp.concatenate([field[owner, part] for owner, part in ROW_BLOCKS], axis=0)
-        hi, lo = split(full.T)
-        both = jnp.concatenate([hi, lo], axis=0)
+        turned = full.T
+        peak = jnp.max(jnp.max(jnp.abs(turned), axis=0, keepdims=True), axis=1, keepdims=True)
+        peak = jnp.maximum(peak, 1e-30)
+        scaled = turned * (PEAK / peak)
+        hi, lo = split_low(scaled)
+        low = jnp.concatenate([lo, scaled.astype(f8)], axis=1)
+        unscale = jnp.broadcast_to(peak * (1.0 / PEAK), (1, LANES))
 
         @pl.loop(0, BLOCKS)
         def _(block):
             for row in range(ROWS):
                 lanes = slice(row * LANES, row * LANES + LANES)
-                first = mm(both, wx[block, 0:256, lanes])
-                second = mm(both[0:256], wx[block, 256:512, lanes])
-                values = first[0:256] + first[256:512] + second
+                values = mm(hi, wx[block, :, lanes]) + mm(low, w8[block, :, lanes]) * (1.0 / LOW)
                 weight = wy[block, :, lanes]
-                a_send[block, 0, row : row + 1, :] = jnp.sum(
+                a_send[block, 0, row : row + 1, :] = unscale * jnp.sum(
                     values[0:128] * weight, axis=0, keepdims=True
                 )
-                a_send[block, 1, row : row + 1, :] = jnp.sum(
+                a_send[block, 1, row : row + 1, :] = unscale * jnp.sum(
                     values[128:256] * weight, axis=0, keepdims=True
                 )
             a_copy(block).start()
@@ -373,12 +387,13 @@
                 values = jnp.concatenate(
                     [weight * cos[row : row + 1, :], -weight * sin[row : row + 1, :]], axis=0
                 )
-                hi, lo = split(values)
+                hi, lo = split_low(values)
                 v_hi[:, lanes] = hi
                 v_lo[:, lanes] = lo
-            first = mm_nt(wx[block], v_hi[...])
-            second = mm_nt(wx[block, 0:256], v_lo[...])
-            current[...] += first[0:256] + first[256:512] + second
+                v_top[:, lanes] = values.astype(f8)
+            current[...] += mm_nt(wx[block], v_hi[...]) + (
+                mm_nt(w8[block, 0:256], v_lo[...]) + mm_nt(w8[block, 256:512], v_top[...])
+            ) * (1.0 / LOW)
 
         if last:
             for part in range(2):
@@ -497,14 +512,16 @@
             pltpu.VMEM((2, 16, 512), f32),
             pltpu.VMEM((2, 2, ROWS, LANES), f32),
             pltpu.VMEM((ITERS, BLOCKS, 6, ROWS, LANES), f32),
-            pltpu.VMEM((BLOCKS, 512, ROWS * LANES), bf16),
+            pltpu.VMEM((BLOCKS, 256, ROWS * LANES), bf16),
             pltpu.VMEM((BLOCKS, 128, ROWS * LANES), f32),
             pltpu.VMEM((8, 2, 16, 256), f32),
             pltpu.VMEM((BLOCKS, 2, ROWS, LANES), f32),
             pltpu.VMEM((BLOCKS, 2, ROWS, LANES), f32),
             pltpu.VMEM((BLOCKS, 2, ROWS, LANES), f32),
             pltpu.VMEM((256, ROWS * LANES), bf16),
-            pltpu.VMEM((256, ROWS * LANES), bf16),
+            pltpu.VMEM((256, ROWS * LANES), f8),
+            pltpu.VMEM((256, ROWS * LANES), f8),
+            pltpu.VMEM((BLOCKS, 512, ROWS * LANES), f8),
             pltpu.VMEM((256, 256), f32),
             pltpu.VMEM((2, 256, 512), bf16),
             pltpu.VMEM((2, 512, 512), bf16),
@@ -532,7 +549,7 @@
             dma((6,)),
         ],
         compiler_params=pltpu.CompilerParams(
-            collective_id=0, has_side_effects=True, vmem_limit_bytes=48 * 1024 * 1024
+            collective_id=0, has_side_effects=True, vmem_limit_bytes=63 * 1024 * 1024
         ),
     )(radiation, electrons, cell_index, cell_offset, kernel_x, kernel_y)
 

time: 107 us -> 96.1 us (0.90)
  Pallas kernels: 99.5 us -> 93.2 us
  local copies, waits for them, and re-layouts: 6.43 us -> 2.1 us
    pallas_call x1, Pallas kernels: 99.5 us -> 93.2 us  [shards(): pl.pallas_call(kernel, out_shape=(jax.ShapeDtypeStruct(radiation.shape, f...]
    unnamed x14 -> x4, local copies, waits for them, and re-layouts: 6.43 us -> 2.1 us
where the time goes in v4:
time: 96.1 us; the launch traced here: 96 us
  Pallas kernels  93.2 us (97%)
  local copies, waits for them, and re-layouts  2.1 us (2%)
    pallas_call x1, Pallas kernels, shards(): pl.pallas_call(kernel, out_shape=(jax.ShapeDtypeStruct(radiation.shape, f...  93.2 us
    unnamed x4, local copies, waits for them, and re-layouts  2.1 us

profile of v4, /device:TPU:1, one launch (start us, length us, event | category | flops | bytes accessed | tf_op | source)
XLA Modules:
  0.0 96.0 jit_solution(5387777413341262199)
XLA Ops:
  0.6 93.2 %shard_map.77 = (f32[16,2,512]{2,1,0:T(2,128)}, f32[2,2,2048]{2,1,0:T(2,128)}) custom-call(f32[16,2,512]{2,1,0:T(2,128)} %radiation_hbm.1, f32[2,2,2048]{2,1,0:T(2,128)} %electrons_hbm.1, s32[2,2,2048]{2,1,0:T(2,128)} %cell_index_hbm.1, f32[2,2,2048]{2,1,0:T(2,128)} %cell_offset_hbm.1, f32[2,256,256]{2,1,0:T(8,128)} %kx_hbm.1, f32[2,256,256]{2,1,0:T(8,128)} %ky_hbm.1), custom_call_target="tpu_custom_call" | custom-call | tf_op jit(solution)/shard_map/pallas_call | solution.py:495
  93.8 0.0 copy-start
  93.9 1.5 %copy.10 = f32[16,2,512]{2,1,0:T(2,128)} copy(f32[16,2,512]{2,1,0:T(2,128)} %get-tuple-element.4) | data formatting | bytes 131072
  95.3 0.0 copy-done
  95.3 0.6 copy.11
Async XLA Ops:
  93.8 1.5 %copy-start = (f32[2,2,2048]{2,1,0:T(2,128)S(1)}, f32[2,2,2048]{2,1,0:T(2,128)}, u32[]{:S(2)}) copy-start(f32[2,2,2048]{2,1,0:T(2,128)} %get-tuple-element.5) | copy-start | bytes 98308

commit v5 on v4

--- a/solution.py
+++ b/solution.py
@@ -18,6 +18,7 @@
 BLOCKS = 4
 ROWS = 8
 LANES = 256
+SEND_ORDER = (6, 7, 2, 3, 4, 5, 1)
 LOW = 4096.0
 PEAK = 32.0
 ROW_BLOCKS = [
@@ -128,8 +129,11 @@
     def peer_device(other):
         return role_device(number, other // 4, other // 2 % 2, other % 2)
 
-    peers = [peer_device((q + step) % 8) for step in range(8)]
-    beside = peer_device(q + 1 - 2 * core)
+    owners = [
+        ((w + key // 4) % 2 * 2 + (u + key // 2) % 2) * 2 + (core + key) % 2 for key in range(8)
+    ]
+    peers = [peer_device(owner) for owner in owners]
+    beside = peers[1]
     ahead = role_device((number + SLICES - 1) % SLICES, w, u, core)
 
     def remote(src, dst, ssem, rsem, device):
@@ -249,7 +253,7 @@
         load.wait()
     kr, ki = kx[0], kx[1]
     for number_part, part in enumerate(split(jnp.concatenate([kr, ki], axis=1))):
-        k2[number_part] = part
+        k2[number_part * 256 : number_part * 256 + 256] = part
     for half_in in range(2):
         for half_out in range(2):
             block_re = ky[0, half_in * 128 : half_in * 128 + 128, half_out * 128 : half_out * 128 + 128]
@@ -279,11 +283,11 @@
 
     def sums_copy(step):
         return remote(
-            mixed.at[(q + step) % 8], sums.at[q], rs_send.at[step], rs_sem.at[step], peers[step]
+            mixed.at[owners[step]], sums.at[q], rs_send.at[step], rs_sem.at[step], peers[step]
         )
 
     def start_gather():
-        for step in range(1, 8):
+        for step in SEND_ORDER:
             gather_copy(step).start()
         field[q] = p_send[core]
 
@@ -313,6 +317,15 @@
             out_send.at[2 + part],
             out_sem.at[2 + last_number % 2],
             home_device(last_number, w, part, u, core),
+        )
+
+    def out_rows(part):
+        return (
+            p_out.at[part],
+            rad_back.at[row_number % 2],
+            out_send.at[part],
+            out_sem.at[row_number % 2],
+            home_device(row_number, w, part, u, core),
         )
 
     def build(n):
@@ -342,8 +355,8 @@
     def advance(n, last):
         if not last:
             place_copy(n).start()
-        for step in range(1, 8):
-            received(field.at[(q + 8 - step) % 8], ag_sem.at[step])
+        for step in SEND_ORDER:
+            received(field.at[owners[step]], ag_sem.at[step])
         full = jnp.concatenate([field[owner, part] for owner, part in ROW_BLOCKS], axis=0)
         turned = full.T
         peak = jnp.max(jnp.max(jnp.abs(turned), axis=0, keepdims=True), axis=1, keepdims=True)
@@ -404,12 +417,15 @@
         re, im = total[:, 0:128], total[:, 128:256]
         stacked = jnp.concatenate([total, jnp.concatenate([-im, re], axis=1)], axis=0)
         hi, lo = split(stacked)
-        product = mm(k2[0], hi) + mm(k2[1], hi) + mm(k2[0], lo)
+        product = mm(k2[...], hi)
+        product = product[0:256] + product[256:512] + mm(k2[0:256], lo)
         for index, (owner, part) in enumerate(ROW_BLOCKS):
             mixed[owner, part] = product[index * 16 : index * 16 + 16]
-        for step in range(1, 8):
+        for step in SEND_ORDER:
             sums_copy(step).start()
         sums[q] = mixed[q]
+        for step in SEND_ORDER:
+            gather_copy(step).wait_send()
         if not last:
             received(el.at[n + 1, :, 2:6], place_sem.at[n])
 
@@ -418,31 +434,32 @@
                 received(el.at[n + 1, block, 0:2], state_sem.at[n, block])
 
             build(n + 1)
-        for step in range(1, 8):
-            received(sums.at[(q + 8 - step) % 8], rs_sem.at[step])
+        for step in SEND_ORDER:
+            received(sums.at[owners[step]], rs_sem.at[step])
         halves = [
             ((sums[half] + sums[half + 2]) + (sums[half + 4] + sums[half + 6])).reshape(32, 256)
             for half in range(2)
         ]
         hi, lo = split(jnp.concatenate(halves, axis=1))
-        result = mm(hi, big_y[0]) + mm(hi, big_y[1]) + mm(lo, big_y[0])
+        result = mm(jnp.concatenate([hi, lo], axis=0), big_y[0])
+        result = result[0:32] + result[32:64] + mm(hi, big_y[1])
         result = jnp.where((number + n + 1) % SLICES == 0, 0.0, result)
-        for step in range(1, 8):
-            gather_copy(step).wait_send()
-            sums_copy(step).wait_send()
         if last:
             p_out[...] = jnp.concatenate(
                 [result[:, 0:128], result[:, 256:384], result[:, 128:256], result[:, 384:512]],
                 axis=1,
             ).reshape(p_out.shape)
+            for part in range(2):
+                send(*out_rows(part))
         else:
             for half in range(2):
                 p_send[half] = result[:, half * 256 : half * 256 + 256].reshape(2, 16, 256)
             start_gather()
             place_copy(n).wait_send()
 
-        @pl.loop(0, BLOCKS)
-        def _(block):
+        for step in SEND_ORDER:
+            sums_copy(step).wait_send()
+        for block in range(BLOCKS):
             a_copy(block).wait_send()
             if not last:
                 state_copy(n, block).wait_send()
@@ -460,17 +477,6 @@
 
     advance(ITERS - 1, True)
 
-    def out_rows(part):
-        return (
-            p_out.at[part],
-            rad_back.at[row_number % 2],
-            out_send.at[part],
-            out_sem.at[row_number % 2],
-            home_device(row_number, w, part, u, core),
-        )
-
-    for part in range(2):
-        send(*out_rows(part))
     for args in starts:
         sent(*args)
     for part in range(2):
@@ -523,7 +529,7 @@
             pltpu.VMEM((256, ROWS * LANES), f8),
             pltpu.VMEM((BLOCKS, 512, ROWS * LANES), f8),
             pltpu.VMEM((256, 256), f32),
-            pltpu.VMEM((2, 256, 512), bf16),
+            pltpu.VMEM((512, 512), bf16),
             pltpu.VMEM((2, 512, 512), bf16),
             pltpu.VMEM((8, 2, 16, 256), f32),
             pltpu.VMEM((8, 2, 16, 256), f32),

time: 96.1 us -> 94.8 us (0.986)
  Pallas kernels: 93.2 us -> 91.9 us
    pallas_call x1, Pallas kernels: 93.2 us -> 91.9 us  [shards(): pl.pallas_call(kernel, out_shape=(jax.ShapeDtypeStruct(radiation.shape, f...]
where the time goes in v5:
time: 94.8 us; the launch traced here: 94.7 us
  Pallas kernels  91.9 us (97%)
  local copies, waits for them, and re-layouts  2.1 us (2%)
    pallas_call x1, Pallas kernels, shards(): pl.pallas_call(kernel, out_shape=(jax.ShapeDtypeStruct(radiation.shape, f...  91.9 us
    unnamed x4, local copies, waits for them, and re-layouts  2.1 us

profile of v5, /device:TPU:1, one launch (start us, length us, event | category | flops | bytes accessed | tf_op | source)
XLA Modules:
  0.0 94.7 jit_solution(1494905942970300424)
XLA Ops:
  0.6 91.9 %shard_map.77 = (f32[16,2,512]{2,1,0:T(2,128)}, f32[2,2,2048]{2,1,0:T(2,128)}) custom-call(f32[16,2,512]{2,1,0:T(2,128)} %radiation_hbm.1, f32[2,2,2048]{2,1,0:T(2,128)} %electrons_hbm.1, s32[2,2,2048]{2,1,0:T(2,128)} %cell_index_hbm.1, f32[2,2,2048]{2,1,0:T(2,128)} %cell_offset_hbm.1, f32[2,256,256]{2,1,0:T(8,128)} %kx_hbm.1, f32[2,256,256]{2,1,0:T(8,128)} %ky_hbm.1), custom_call_target="tpu_custom_call" | custom-call | tf_op jit(solution)/shard_map/pallas_call | solution.py:501
  92.6 0.0 copy-start
  92.6 1.5 %copy.10 = f32[16,2,512]{2,1,0:T(2,128)} copy(f32[16,2,512]{2,1,0:T(2,128)} %get-tuple-element.4) | data formatting | bytes 131072
  94.1 0.0 copy-done
  94.1 0.6 copy.11
Async XLA Ops:
  92.6 1.5 %copy-start = (f32[2,2,2048]{2,1,0:T(2,128)S(1)}, f32[2,2,2048]{2,1,0:T(2,128)}, u32[]{:S(2)}) copy-start(f32[2,2,2048]{2,1,0:T(2,128)} %get-tuple-element.5) | copy-start | bytes 98308

commit v6 on v5

--- a/solution.py
+++ b/solution.py
@@ -30,9 +30,9 @@
 ]
 
 
-def split(value):
+def split(value, scale=1.0):
     hi = value.astype(bf16)
-    return hi, (value - hi.astype(f32)).astype(bf16)
+    return hi, ((value - hi.astype(f32)) * scale).astype(bf16)
 
 
 def split_low(value):
@@ -328,27 +328,34 @@
             home_device(row_number, w, part, u, core),
         )
 
-    def build(n):
+    def build(n, first):
         @pl.loop(0, BLOCKS)
         def _(block):
+            if first:
+                received(el.at[0, block], el_sem.at[block])
+            grid_x = lax.broadcasted_iota(jnp.int32, (256, LANES), 0).astype(f32).astype(bf16)
+            grid_y = (lax.broadcasted_iota(jnp.int32, (128, LANES), 0) + core * 128).astype(f32)
+            none = jnp.zeros((256, LANES), bf16)
             for row in range(ROWS):
                 index_x = el[n, block, 2, row : row + 1, :]
                 index_y = el[n, block, 3, row : row + 1, :]
                 offset_x = el[n, block, 4, row : row + 1, :]
                 offset_y = el[n, block, 5, row : row + 1, :]
                 lanes = slice(row * LANES, row * LANES + LANES)
-                grid_x = lax.broadcasted_iota(jnp.int32, (256, LANES), 0).astype(f32)
-                grid_y = (lax.broadcasted_iota(jnp.int32, (128, LANES), 0) + core * 128).astype(f32)
-                weight = jnp.where(grid_x == index_x, 1.0 - offset_x, 0.0) + jnp.where(
-                    grid_x == index_x + 1.0, offset_x, 0.0
+                lower, lower_low = split(1.0 - offset_x, LOW)
+                upper, upper_low = split(offset_x, LOW)
+                at_lower = grid_x == index_x.astype(bf16)
+                at_upper = grid_x == (index_x + 1.0).astype(bf16)
+                hi = jnp.where(at_lower, lower, jnp.where(at_upper, upper, none))
+                lo = jnp.where(at_lower, lower_low, jnp.where(at_upper, upper_low, none))
+                wx[block, 0:256, lanes] = hi
+                w8[block, 0:256, lanes] = hi.astype(f8)
+                w8[block, 256:512, lanes] = lo.astype(f8)
+                wy[block, :, lanes] = jnp.where(
+                    grid_y == index_y,
+                    1.0 - offset_y,
+                    jnp.where(grid_y == index_y + 1.0, offset_y, 0.0),
                 )
-                hi, lo = split_low(weight)
-                wx[block, 0:256, lanes] = hi
-                w8[block, 0:256, lanes] = weight.astype(f8)
-                w8[block, 256:512, lanes] = lo
-                wy[block, :, lanes] = jnp.where(
-                    grid_y == index_y, 1.0 - offset_y, 0.0
-                ) + jnp.where(grid_y == index_y + 1.0, offset_y, 0.0)
             trig[block, 0] = jnp.cos(el[n, block, 0])
             trig[block, 1] = jnp.sin(el[n, block, 0])
 
@@ -433,7 +440,7 @@
             def _(block):
                 received(el.at[n + 1, block, 0:2], state_sem.at[n, block])
 
-            build(n + 1)
+            build(n + 1, False)
         for step in SEND_ORDER:
             received(sums.at[owners[step]], rs_sem.at[step])
         halves = [
@@ -467,9 +474,7 @@
     for part in range(2):
         received(p_send.at[:, part], row_sem.at[part])
     start_gather()
-    for slot in range(BLOCKS):
-        received(el.at[0, slot], el_sem.at[slot])
-    build(0)
+    build(0, True)
 
     @pl.loop(0, ITERS - 1)
     def _(n):

time: 94.8 us -> 92.9 us (0.980)
  Pallas kernels: 91.9 us -> 90 us
    pallas_call x1, Pallas kernels: 91.9 us -> 90 us  [shards(): pl.pallas_call(kernel, out_shape=(jax.ShapeDtypeStruct(radiation.shape, f...]
where the time goes in v6:
time: 92.9 us; the launch traced here: 92.8 us
  Pallas kernels  90 us (97%)
  local copies, waits for them, and re-layouts  2.1 us (2%)
    pallas_call x1, Pallas kernels, shards(): pl.pallas_call(kernel, out_shape=(jax.ShapeDtypeStruct(radiation.shape, f...  90 us
    unnamed x4, local copies, waits for them, and re-layouts  2.1 us

profile of v6, /device:TPU:1, one launch (start us, length us, event | category | flops | bytes accessed | tf_op | source)
XLA Modules:
  0.0 92.8 jit_solution(8677069580209046308)
XLA Ops:
  0.6 90.0 %shard_map.77 = (f32[16,2,512]{2,1,0:T(2,128)}, f32[2,2,2048]{2,1,0:T(2,128)}) custom-call(f32[16,2,512]{2,1,0:T(2,128)} %radiation_hbm.1, f32[2,2,2048]{2,1,0:T(2,128)} %electrons_hbm.1, s32[2,2,2048]{2,1,0:T(2,128)} %cell_index_hbm.1, f32[2,2,2048]{2,1,0:T(2,128)} %cell_offset_hbm.1, f32[2,256,256]{2,1,0:T(8,128)} %kx_hbm.1, f32[2,256,256]{2,1,0:T(8,128)} %ky_hbm.1), custom_call_target="tpu_custom_call" | custom-call | tf_op jit(solution)/shard_map/pallas_call | solution.py:506
  90.7 0.0 copy-start
  90.7 1.5 %copy.10 = f32[16,2,512]{2,1,0:T(2,128)} copy(f32[16,2,512]{2,1,0:T(2,128)} %get-tuple-element.4) | data formatting | bytes 131072
  92.1 0.0 copy-done
  92.2 0.6 copy.11
Async XLA Ops:
  90.7 1.5 %copy-start = (f32[2,2,2048]{2,1,0:T(2,128)S(1)}, f32[2,2,2048]{2,1,0:T(2,128)}, u32[]{:S(2)}) copy-start(f32[2,2,2048]{2,1,0:T(2,128)} %get-tuple-element.5) | copy-start | bytes 98308

commit v7 on v6

--- a/solution.py
+++ b/solution.py
@@ -560,9 +560,14 @@
             dma((6,)),
         ],
         compiler_params=pltpu.CompilerParams(
-            collective_id=0, has_side_effects=True, vmem_limit_bytes=63 * 1024 * 1024
+            collective_id=0, has_side_effects=True, vmem_limit_bytes=48 * 1024 * 1024
         ),
-    )(radiation, electrons, cell_index, cell_offset, kernel_x, kernel_y)
+    )(
+        *[
+            pltpu.with_memory_space_constraint(array, pltpu.HBM)
+            for array in (radiation, electrons, cell_index, cell_offset, kernel_x, kernel_y)
+        ]
+    )
 
 
 def solution(mesh):

time: 92.9 us -> 91.4 us (0.984)
    unnamed x4 -> x2, local copies, waits for them, and re-layouts: 2.1 us -> 1.25 us
where the time goes in v7:
time: 91.4 us; the launch traced here: 91.3 us
  Pallas kernels  89.4 us (98%)
  local copies, waits for them, and re-layouts  1.25 us (1%)
    pallas_call x1, Pallas kernels, shards(): pl.pallas_call(kernel, out_shape=(jax.ShapeDtypeStruct(radiation.shape, f...  89.4 us

profile of v7, /device:TPU:1, one launch (start us, length us, event | category | flops | bytes accessed | tf_op | source)
XLA Modules:
  0.0 91.3 jit_solution(13128374853905615873)
XLA Ops:
  0.6 89.4 %shard_map.77 = (f32[16,2,512]{2,1,0:T(2,128)S(1)}, f32[2,2,2048]{2,1,0:T(2,128)S(1)}) custom-call(f32[16,2,512]{2,1,0:T(2,128)} %radiation_hbm.1, f32[2,2,2048]{2,1,0:T(2,128)} %electrons_hbm.1, s32[2,2,2048]{2,1,0:T(2,128)} %cell_index_hbm.1, f32[2,2,2048]{2,1,0:T(2,128)} %cell_offset_hbm.1, f32[2,256,256]{2,1,0:T(8,128)} %kx_hbm.1, f32[2,256,256]{2,1,0:T(8,128)} %ky_hbm.1), custom_call_target="tpu_custom_call" | custom-call | tf_op jit(solution)/shard_map/pallas_call | solution.py:506
  90.0 0.6 copy.10
  90.7 0.6 copy.11

commit v8 on v7

--- a/solution.py
+++ b/solution.py
@@ -203,8 +203,7 @@
     ]
     for load in loads:
         load.start()
-    for load in loads[0:4]:
-        load.wait()
+    loads[0].wait()
     for p in range(2):
         for half in range(2):
             for part in range(2):
@@ -212,15 +211,6 @@
                 rad[p, half, :, part * 128 : part * 128 + 128] = radiation[
                     :, p, column : column + 128
                 ]
-        for row in range(ROWS):
-            lanes = slice(row * LANES, row * LANES + LANES)
-            for field_number in range(2):
-                place = slice(row, row + 1)
-                el_in[p, field_number, place] = electrons[field_number, p : p + 1, lanes]
-                el_in[p, 2 + field_number, place] = cell_index[
-                    field_number, p : p + 1, lanes
-                ].astype(f32)
-                el_in[p, 4 + field_number, place] = cell_offset[field_number, p : p + 1, lanes]
     pl.semaphore_wait(barrier, expected)
 
     own_slot = y_hi * 2 + core
@@ -235,6 +225,20 @@
                 role_device(2 * cuts + p, x_hi, u, core),
             )
         )
+    for args in starts:
+        send(*args)
+    for load in loads[1:4]:
+        load.wait()
+    for p in range(2):
+        for row in range(ROWS):
+            lanes = slice(row * LANES, row * LANES + LANES)
+            for field_number in range(2):
+                place = slice(row, row + 1)
+                el_in[p, field_number, place] = electrons[field_number, p : p + 1, lanes]
+                el_in[p, 2 + field_number, place] = cell_index[
+                    field_number, p : p + 1, lanes
+                ].astype(f32)
+                el_in[p, 4 + field_number, place] = cell_offset[field_number, p : p + 1, lanes]
     for p in range(2):
         for number_core in range(2):
             starts.append(
@@ -246,7 +250,7 @@
                     role_device(2 * cuts + p, x_hi, u, (core + number_core) % 2),
                 )
             )
-    for args in starts:
+    for args in starts[2:]:
         send(*args)
 
     for load in loads[4:6]:
@@ -359,9 +363,13 @@
             trig[block, 0] = jnp.cos(el[n, block, 0])
             trig[block, 1] = jnp.sin(el[n, block, 0])
 
-    def advance(n, last):
-        if not last:
+    def advance(n):
+        moving = n < ITERS - 1
+
+        @pl.when(moving)
+        def _():
             place_copy(n).start()
+
         for step in SEND_ORDER:
             received(field.at[owners[step]], ag_sem.at[step])
         full = jnp.concatenate([field[owner, part] for owner, part in ROW_BLOCKS], axis=0)
@@ -370,14 +378,15 @@
         peak = jnp.maximum(peak, 1e-30)
         scaled = turned * (PEAK / peak)
         hi, lo = split_low(scaled)
+        hi = (hi.astype(f32) * LOW).astype(bf16)
         low = jnp.concatenate([lo, scaled.astype(f8)], axis=1)
-        unscale = jnp.broadcast_to(peak * (1.0 / PEAK), (1, LANES))
+        unscale = jnp.broadcast_to(peak * (1.0 / (PEAK * LOW)), (1, LANES))
 
         @pl.loop(0, BLOCKS)
         def _(block):
             for row in range(ROWS):
                 lanes = slice(row * LANES, row * LANES + LANES)
-                values = mm(hi, wx[block, :, lanes]) + mm(low, w8[block, :, lanes]) * (1.0 / LOW)
+                values = mm(hi, wx[block, :, lanes]) + mm(low, w8[block, :, lanes])
                 weight = wy[block, :, lanes]
                 a_send[block, 0, row : row + 1, :] = unscale * jnp.sum(
                     values[0:128] * weight, axis=0, keepdims=True
@@ -398,8 +407,11 @@
             phase = el[n, block, 0] + phase_step * energy
             el[n, block, 0] = phase
             el[n, block, 1] = energy
-            if not last:
+
+            @pl.when(moving)
+            def _():
                 state_copy(n, block).start()
+
             cos, sin = jnp.cos(phase), jnp.sin(phase)
             for row in range(ROWS):
                 lanes = slice(row * LANES, row * LANES + LANES)
@@ -415,7 +427,8 @@
                 mm_nt(w8[block, 0:256], v_lo[...]) + mm_nt(w8[block, 256:512], v_top[...])
             ) * (1.0 / LOW)
 
-        if last:
+        @pl.when(jnp.logical_not(moving))
+        def _():
             for part in range(2):
                 el_send[part] = el[n, part * 2 + core, 0:2]
                 send(*out_electrons(part))
@@ -433,7 +446,8 @@
         sums[q] = mixed[q]
         for step in SEND_ORDER:
             gather_copy(step).wait_send()
-        if not last:
+        @pl.when(moving)
+        def _():
             received(el.at[n + 1, :, 2:6], place_sem.at[n])
 
             @pl.loop(0, BLOCKS)
@@ -451,14 +465,16 @@
         result = mm(jnp.concatenate([hi, lo], axis=0), big_y[0])
         result = result[0:32] + result[32:64] + mm(hi, big_y[1])
         result = jnp.where((number + n + 1) % SLICES == 0, 0.0, result)
-        if last:
+        @pl.when(jnp.logical_not(moving))
+        def _():
             p_out[...] = jnp.concatenate(
                 [result[:, 0:128], result[:, 256:384], result[:, 128:256], result[:, 384:512]],
                 axis=1,
             ).reshape(p_out.shape)
             for part in range(2):
                 send(*out_rows(part))
-        else:
+        @pl.when(moving)
+        def _():
             for half in range(2):
                 p_send[half] = result[:, half * 256 : half * 256 + 256].reshape(2, 16, 256)
             start_gather()
@@ -468,7 +484,9 @@
             sums_copy(step).wait_send()
         for block in range(BLOCKS):
             a_copy(block).wait_send()
-            if not last:
+
+            @pl.when(moving)
+            def _():
                 state_copy(n, block).wait_send()
 
     for part in range(2):
@@ -476,11 +494,9 @@
     start_gather()
     build(0, True)
 
-    @pl.loop(0, ITERS - 1)
+    @pl.loop(0, ITERS)
     def _(n):
-        advance(n, False)
-
-    advance(ITERS - 1, True)
+        advance(n)
 
     for args in starts:
         sent(*args)

time: 91.4 us -> 91.6 us (level)
  no operation moved by 1% of the time
where the time goes in v8:
time: 91.6 us; the launch traced here: 91.5 us
  Pallas kernels  89.6 us (98%)
  local copies, waits for them, and re-layouts  1.25 us (1%)
    pallas_call x1, Pallas kernels, shards(): pl.pallas_call(kernel, out_shape=(jax.ShapeDtypeStruct(radiation.shape, f...  89.6 us

profile of v8, /device:TPU:1, one launch (start us, length us, event | category | flops | bytes accessed | tf_op | source)
XLA Modules:
  0.0 91.5 jit_solution(1366982708308386069)
XLA Ops:
  0.6 89.6 %shard_map.77 = (f32[16,2,512]{2,1,0:T(2,128)S(1)}, f32[2,2,2048]{2,1,0:T(2,128)S(1)}) custom-call(f32[16,2,512]{2,1,0:T(2,128)} %radiation_hbm.1, f32[2,2,2048]{2,1,0:T(2,128)} %electrons_hbm.1, s32[2,2,2048]{2,1,0:T(2,128)} %cell_index_hbm.1, f32[2,2,2048]{2,1,0:T(2,128)} %cell_offset_hbm.1, f32[2,256,256]{2,1,0:T(8,128)} %kx_hbm.1, f32[2,256,256]{2,1,0:T(8,128)} %ky_hbm.1), custom_call_target="tpu_custom_call" | custom-call | tf_op jit(solution)/shard_map/pallas_call | solution.py:522
  90.2 0.6 copy.10
  90.9 0.6 copy.11

commit v9 on v7

--- a/solution.py
+++ b/solution.py
@@ -359,9 +359,13 @@
             trig[block, 0] = jnp.cos(el[n, block, 0])
             trig[block, 1] = jnp.sin(el[n, block, 0])
 
-    def advance(n, last):
-        if not last:
+    def advance(n):
+        moving = n < ITERS - 1
+
+        @pl.when(moving)
+        def _():
             place_copy(n).start()
+
         for step in SEND_ORDER:
             received(field.at[owners[step]], ag_sem.at[step])
         full = jnp.concatenate([field[owner, part] for owner, part in ROW_BLOCKS], axis=0)
@@ -398,8 +402,11 @@
             phase = el[n, block, 0] + phase_step * energy
             el[n, block, 0] = phase
             el[n, block, 1] = energy
-            if not last:
+
+            @pl.when(moving)
+            def _():
                 state_copy(n, block).start()
+
             cos, sin = jnp.cos(phase), jnp.sin(phase)
             for row in range(ROWS):
                 lanes = slice(row * LANES, row * LANES + LANES)
@@ -415,7 +422,8 @@
                 mm_nt(w8[block, 0:256], v_lo[...]) + mm_nt(w8[block, 256:512], v_top[...])
             ) * (1.0 / LOW)
 
-        if last:
+        @pl.when(jnp.logical_not(moving))
+        def _():
             for part in range(2):
                 el_send[part] = el[n, part * 2 + core, 0:2]
                 send(*out_electrons(part))
@@ -433,7 +441,8 @@
         sums[q] = mixed[q]
         for step in SEND_ORDER:
             gather_copy(step).wait_send()
-        if not last:
+        @pl.when(moving)
+        def _():
             received(el.at[n + 1, :, 2:6], place_sem.at[n])
 
             @pl.loop(0, BLOCKS)
@@ -451,14 +460,16 @@
         result = mm(jnp.concatenate([hi, lo], axis=0), big_y[0])
         result = result[0:32] + result[32:64] + mm(hi, big_y[1])
         result = jnp.where((number + n + 1) % SLICES == 0, 0.0, result)
-        if last:
+        @pl.when(jnp.logical_not(moving))
+        def _():
             p_out[...] = jnp.concatenate(
                 [result[:, 0:128], result[:, 256:384], result[:, 128:256], result[:, 384:512]],
                 axis=1,
             ).reshape(p_out.shape)
             for part in range(2):
                 send(*out_rows(part))
-        else:
+        @pl.when(moving)
+        def _():
             for half in range(2):
                 p_send[half] = result[:, half * 256 : half * 256 + 256].reshape(2, 16, 256)
             start_gather()
@@ -468,7 +479,9 @@
             sums_copy(step).wait_send()
         for block in range(BLOCKS):
             a_copy(block).wait_send()
-            if not last:
+
+            @pl.when(moving)
+            def _():
                 state_copy(n, block).wait_send()
 
     for part in range(2):
@@ -476,11 +489,9 @@
     start_gather()
     build(0, True)
 
-    @pl.loop(0, ITERS - 1)
+    @pl.loop(0, ITERS)
     def _(n):
-        advance(n, False)
-
-    advance(ITERS - 1, True)
+        advance(n)
 
     for args in starts:
         sent(*args)

time: 91.4 us -> 91.4 us (level)
  no operation moved by 1% of the time
where the time goes in v9:
time: 91.4 us; the launch traced here: 91.3 us
  Pallas kernels  89.4 us (98%)
  local copies, waits for them, and re-layouts  1.25 us (1%)
    pallas_call x1, Pallas kernels, shards(): pl.pallas_call(kernel, out_shape=(jax.ShapeDtypeStruct(radiation.shape, f...  89.4 us

profile of v9, /device:TPU:1, one launch (start us, length us, event | category | flops | bytes accessed | tf_op | source)
XLA Modules:
  0.0 91.3 jit_solution(4677737720184559002)
XLA Ops:
  0.6 89.4 %shard_map.77 = (f32[16,2,512]{2,1,0:T(2,128)S(1)}, f32[2,2,2048]{2,1,0:T(2,128)S(1)}) custom-call(f32[16,2,512]{2,1,0:T(2,128)} %radiation_hbm.1, f32[2,2,2048]{2,1,0:T(2,128)} %electrons_hbm.1, s32[2,2,2048]{2,1,0:T(2,128)} %cell_index_hbm.1, f32[2,2,2048]{2,1,0:T(2,128)} %cell_offset_hbm.1, f32[2,256,256]{2,1,0:T(8,128)} %kx_hbm.1, f32[2,256,256]{2,1,0:T(8,128)} %ky_hbm.1), custom_call_target="tpu_custom_call" | custom-call | tf_op jit(solution)/shard_map/pallas_call | solution.py:517
  90.0 0.6 copy.10
  90.7 0.6 copy.11
